TPU v7x, 32 devices: a whole 2x2x4 slice. The times are simulated.
32 devices in a mesh: tile: 8 (over z, x), mem: 4 (over y, core).
Axes of the slice: x: 2, y: 2, z: 4, core: 2. Of those that a mesh axis runs over, the one named last changes fastest.
Arguments:
- prior_ensemble_fields: float32 [128, 32, 512], P('mem', 'tile'), may hold values from -6 to 6
- vel_y: float32 [32, 512], P('tile'), may hold values from -0.4 to 0.4
- vel_x: float32 [32, 512], P('tile'), may hold values from -0.4 to 0.4
- diffus: float32 [32, 512], P('tile'), may hold values from 0.02 to 0.2
- assign: int32 [8, 2048], P('tile'), may hold values from 0 to 2047, each once within a row
- obs_cell: int32 [64, 512], P(('tile', 'mem')), may hold values from 0 to 255
- obs_value: float32 [64, 512], P(('tile', 'mem')), may hold values from -6 to 6
- obs_var: float32 [64, 512], P(('tile', 'mem')), may hold values from 0.2 to 2
Outputs:
- analysis: float32 [128, 32, 512], P('mem', 'tile')
All inputs are finite; a program needn't handle non-finite values.
Results may differ from a plain program's by a relative error of at most 0.0003.
Values sent between devices are 32-bit elements; how exact they have to be, the bound alone decides.
A program may use at most 64 MiB of HBM per device.

v0:
```python
import jax
import jax.numpy as jnp
from jax import lax
from jax.sharding import PartitionSpec as P

PATCH = 256


def extended(block, sides, width):
    for axis, dim in sides:
        count = lax.axis_size(axis)
        forward = [(i, i + 1) for i in range(count - 1)]
        backward = [(target, source) for source, target in forward]
        low = lax.ppermute(
            lax.slice_in_dim(block, block.shape[dim] - width, None, axis=dim), axis, forward
        )
        high = lax.ppermute(lax.slice_in_dim(block, 0, width, axis=dim), axis, backward)
        block = jnp.concatenate([low, block, high], axis=dim)
    return block


def advance(padded, coef_y, coef_x, coef_k):
    center = padded[..., 2:-2, :]
    above = padded[..., 3:-1, :]
    below = padded[..., 1:-3, :]
    grad_y = (-padded[..., 4:, :] + 8.0 * above - 8.0 * below + padded[..., :-4, :]) / 12.0
    lap_y = above - 2.0 * center + below
    right_one = jnp.roll(center, -1, axis=-1)
    left_one = jnp.roll(center, 1, axis=-1)
    grad_x = (
        -jnp.roll(center, -2, axis=-1)
        + 8.0 * right_one
        - 8.0 * left_one
        + jnp.roll(center, 2, axis=-1)
    ) / 12.0
    lap_x = right_one - 2.0 * center + left_one
    return center - coef_y * grad_y - coef_x * grad_x + coef_k * (lap_y + lap_x)


def analyze(members, cells, observed, variance):
    ensemble_size = members.shape[0]
    highest = lax.Precision.HIGHEST
    center = jnp.mean(members, axis=0)
    spread = members - center[None, :]
    obs_spread = jnp.take(spread, cells, axis=1)
    innovation = observed - jnp.take(center, cells)
    weighted = obs_spread / variance[None, :]
    gram = jnp.dot(weighted, obs_spread.T, precision=highest, preferred_element_type=jnp.float32)
    system = gram + (ensemble_size - 1.0) * jnp.eye(ensemble_size, dtype=jnp.float32)
    factor = jnp.linalg.cholesky(system)
    pulled = jnp.dot(weighted, innovation, precision=highest, preferred_element_type=jnp.float32)
    right_side = jnp.concatenate([pulled[:, None], gram], axis=1)
    solved = jax.scipy.linalg.cho_solve((factor, True), right_side)
    gain_mean = solved[:, 0]
    mixing = solved[:, 1:]
    transform = jnp.eye(ensemble_size, dtype=jnp.float32) - 0.5 * mixing + gain_mean[None, :]
    return center[None, :] + jnp.dot(
        transform, spread, precision=highest, preferred_element_type=jnp.float32
    )


def on_device(prior_ensemble_fields, vel_y, vel_x, diffus, assign, obs_cell, obs_value, obs_var):
    local_members, tile_rows, width_cells = prior_ensemble_fields.shape
    columns = tile_rows * width_cells
    groups = lax.axis_size("mem")
    group_columns = columns // groups
    patches_here = group_columns // PATCH
    ensemble = prior_ensemble_fields
    stacked = jnp.concatenate([ensemble, vel_y[None], vel_x[None], diffus[None]], axis=0)
    widened = extended(stacked, (("tile", 1),), 4)
    field_rows = widened[:local_members]
    near_y = widened[local_members, 2:-2]
    near_x = widened[local_members + 1, 2:-2]
    near_k = widened[local_members + 2, 2:-2]
    middle = advance(field_rows, near_y, near_x, near_k)
    first_row = lax.axis_index("tile") * tile_rows - 2
    global_rows = first_row + jnp.arange(tile_rows + 4, dtype=jnp.int32)
    inside = (global_rows >= 0) & (global_rows < tile_rows * lax.axis_size("tile"))
    middle = jnp.where(inside[None, :, None], middle, 0.0)
    ensemble = advance(middle, vel_y, vel_x, diffus)
    order = assign[0]
    permuted = jnp.take(ensemble.reshape(local_members, columns), order, axis=1)
    blocks = permuted.reshape(local_members, groups, group_columns)
    gathered = lax.all_to_all(blocks, "mem", split_axis=1, concat_axis=0, tiled=True)
    gathered = gathered.reshape(local_members * groups, patches_here, PATCH)
    updated = jax.vmap(analyze, in_axes=(1, 0, 0, 0), out_axes=1)(
        gathered, obs_cell, obs_value, obs_var
    )
    outgoing = updated.reshape(local_members * groups, 1, group_columns)
    returned = lax.all_to_all(outgoing, "mem", split_axis=0, concat_axis=1, tiled=True)
    returned = returned.reshape(local_members, columns)
    positions = jnp.argsort(order)
    analysed = jnp.take(returned, positions, axis=1).reshape(local_members, tile_rows, width_cells)
    padded = extended(analysed, (("tile", 1),), 2)
    return advance(padded, vel_y, vel_x, diffus)


def solution(mesh):
    return jax.shard_map(
        on_device,
        mesh=mesh,
        in_specs=(
            P("mem", "tile", None),
            P("tile", None),
            P("tile", None),
            P("tile", None),
            P("tile", None),
            P(("tile", "mem"), None),
            P(("tile", "mem"), None),
            P(("tile", "mem"), None),
        ),
        out_specs=P("mem", "tile", None),
        check_vma=False,
    )
```

profile of v0, /device:TPU:24, one launch (start us, length us, event | category | flops | bytes accessed | tf_op | source)
XLA Modules:
  0.0 133.3 jit_solution(381985108282282040)
XLA Ops:
  0.0 1.1 pad_maximum_fusion.11
  1.1 3.4 %collective-permute-start = (f32[35,4,512]{2,1,0:T(4,128)S(1)}, f32[35,4,512]{2,1,0:T(4,128)S(1)}, u32[]{:S(2)}, u32[]{:S(2)}) collective-permute-start(f32[35,4,512]{2,1,0:T(4,128)S(1)} %pad_maximum_fusion.11), channel_id=1, source_target_pairs={{0,4},{4,8},{8,12},{12,16},{16,20},{20,24},{24,28},{1,5},{5,9},{9,... | collective-permute-start | bytes 860168 | tf_op jit(solution)/shard_map/ppermute | solution.py:14
  4.5 3.3 %collective-permute-start.1 = (f32[35,4,512]{2,1,0:T(4,128)S(1)}, f32[35,4,512]{2,1,0:T(4,128)S(1)}, u32[]{:S(2)}, u32[]{:S(2)}) collective-permute-start(f32[35,4,512]{2,1,0:T(4,128)S(1)} %pad_maximum_fusion.11), channel_id=1, source_target_pairs={{4,0},{8,4},{12,8},{16,12},{20,16},{24,20},{28,24},{5,1},{9,5},{13... | collective-permute-start | bytes 860168 | tf_op jit(solution)/shard_map/ppermute | solution.py:17
  7.8 0.7 fusion.66
  8.5 0.7 compare_and_fusion.1
  9.3 0.7 fusion.68
  10.0 5.7 %sort.17 = (s32[2048]{0:T(1024)}, s32[2048]{0:T(1024)S(1)}) sort(s32[2048]{0:T(1024)} %bitcast.89, s32[2048]{0:T(1024)S(1)} %iota.82), dimensions={0}, to_apply=%region_3.5 | sort | flops 22528 | bytes 32768 | tf_op jit(solution)/shard_map/jit(argsort)/sort | solution.py:92
  15.8 0.7 broadcast_multiply_fusion
  16.5 2.1 %collective-permute-done.1 = f32[35,4,512]{2,1,0:T(4,128)S(1)} collective-permute-done((f32[35,4,512]{2,1,0:T(4,128)S(1)}, f32[35,4,512]{2,1,0:T(4,128)S(1)}, u32[]{:S(2)}, u32[]{:S(2)}) %collective-permute-start.1) | collective-permute-done | bytes 286752 | tf_op jit(solution)/shard_map/ppermute | solution.py:17
  18.6 1.2 pad_maximum_fusion
  21.1 0.9 fusion.6
  22.6 0.8 fusion.29
  23.7 5.5 %gather_fusion.2 = f32[2048,32]{1,0:T(8,128)S(1)} fusion(f32[32,2048]{0,1:T(8,128)S(1)} %bitcast.66, s32[2048]{0:T(1024)S(1)} %fusion.66), kind=kCustom, calls=%fused_computation.clone | custom fusion | bytes 532480 | tf_op jit(solution)/shard_map/jit(_take)/gather | solution.py:82
  29.6 1.0 copy.82
  30.6 3.6 %all-to-all-start = ((f32[32,4,512]{2,0,1:T(8,128)}), f32[32,4,512]{2,0,1:T(8,128)S(1)}, u32[]{:S(2)}, u32[]{:S(2)}) async-start(f32[32,4,512]{2,0,1:T(8,128)} %copy.82), calls=%async_computation | async-start | bytes 524288 | tf_op jit(solution)/shard_map/all_to_all | solution.py:84
  34.2 5.8 %all-to-all-done = f32[32,4,512]{2,0,1:T(8,128)S(1)} async-done(((f32[32,4,512]{2,0,1:T(8,128)}), f32[32,4,512]{2,0,1:T(8,128)S(1)}, u32[]{:S(2)}, u32[]{:S(2)}) %all-to-all-start) | async-done | bytes 262176 | tf_op jit(solution)/shard_map/all_to_all | solution.py:84
  40.5 9.1 %gather_fusion.1 = f32[1024]{0:T(1024)S(1)} fusion(f32[2,256]{1,0:T(2,128)S(1)} %div.32, s32[1024]{0:T(1024)S(1)} %bitcast.64), kind=kCustom, calls=%fused_computation.3 | custom fusion | bytes 16384 | tf_op jit(solution)/shard_map/vmap(jit(_take))/gather | solution.py:46
  49.6 6.8 %gather_fusion = f32[1024,128]{1,0:T(8,128)S(1)} fusion(f32[2,128,256]{1,2,0:T(8,128)S(1)} %subtract_bitcast_fusion, s32[1024]{0:T(1024)S(1)} %bitcast.65), kind=kCustom, calls=%fused_computation.2 | custom fusion | bytes 1056768 | tf_op jit(solution)/shard_map/vmap(jit(_take))/gather | solution.py:45
  56.5 1.8 %fusion.14 = f32[2,128,128]{1,2,0:T(8,128)S(1)} fusion(f32[2,512,128]{2,1,0:T(8,128)S(1)} %bitcast.73, f32[2,512]{1,0:T(2,128)S(1)} %copy-done.6, pred[2,512]{1,0:T(4,128)(4,1)S(1)} %get-tuple-element.9), kind=kOutput, calls=%fused_computation.38 | convolution fusion | flops 201719808 | bytes 660480 | tf_op jit(solution)/shard_map/vmap()/dot_general | solution.py:48
  58.5 23.5 %custom-call.11 = f32[2,128,128]{2,1,0:T(8,128)S(1)} custom-call(f32[2,128,128]{2,1,0:T(8,128)S(1)} %fusion.54), custom_call_target="Cholesky" | custom-call | tf_op jit(solution)/shard_map/vmap(jit(cholesky))/cholesky | solution.py:50
  82.2 19.7 %custom-call.12 = f32[2,1,128,128]{2,3,1,0:T(8,128)S(1)} custom-call(f32[2,1,128,128]{3,2,1,0:T(8,128)S(1)} %select_bitcast_fusion), custom_call_target="InvertDiagBlocksLowerTriangular" | custom-call | tf_op jit(solution)/shard_map/vmap(jit(_cho_solve))/triangular_solve | solution.py:53
  101.9 0.6 convolution_bitcast_fusion
  103.4 0.5 fusion
  104.0 0.8 copy.91
  104.9 3.4 %all-to-all-start.1 = ((f32[128,1,512]{2,1,0:T(1,128)}), f32[128,1,512]{2,1,0:T(1,128)S(1)}, u32[]{:S(2)}, u32[]{:S(2)}) async-start(f32[128,1,512]{2,1,0:T(1,128)} %copy.91), calls=%async_computation.1 | async-start | bytes 524288 | tf_op jit(solution)/shard_map/all_to_all | solution.py:90
  108.3 6.0 %all-to-all-done.1 = f32[128,1,512]{2,1,0:T(1,128)S(1)} async-done(((f32[128,1,512]{2,1,0:T(1,128)}), f32[128,1,512]{2,1,0:T(1,128)S(1)}, u32[]{:S(2)}, u32[]{:S(2)}) %all-to-all-start.1) | async-done | bytes 262176 | tf_op jit(solution)/shard_map/all_to_all | solution.py:90
  114.6 5.5 %gather_fusion.3 = f32[2048,32]{1,0:T(8,128)S(1)} fusion(f32[32,2048]{0,1:T(8,128)S(1)} %bitcast.67, s32[2048]{0:T(1024)S(1)} %fusion.67), kind=kCustom, calls=%fused_computation.1.clone | custom fusion | bytes 532480 | tf_op jit(solution)/shard_map/jit(_take)/gather | solution.py:93
  121.4 2.4 %collective-permute-start.2 = (f32[32,2,512]{2,1,0:T(2,128)S(1)}, f32[32,2,512]{2,1,0:T(2,128)S(1)}, u32[]{:S(2)}, u32[]{:S(2)}) collective-permute-start(f32[32,2,512]{2,1,0:T(2,128)S(1)} %get-tuple-element.38), channel_id=1, source_target_pairs={{4,0},{8,4},{12,8},{16,12},{20,16},{24,20},{28,24},{5,1},{9,5},{13... | collective-permute-start | bytes 393224 | tf_op jit(solution)/shard_map/ppermute | solution.py:17
  123.8 3.5 %collective-permute-start.3 = (f32[32,2,512]{2,1,0:T(2,128)S(1)}, f32[32,2,512]{2,1,0:T(2,128)S(1)}, u32[]{:S(2)}, u32[]{:S(2)}) collective-permute-start(f32[32,2,512]{2,1,0:T(2,128)S(1)} %get-tuple-element.37), channel_id=1, source_target_pairs={{0,4},{4,8},{8,12},{12,16},{16,20},{20,24},{24,28},{1,5},{5,9},{9,... | collective-permute-start | bytes 393224 | tf_op jit(solution)/shard_map/ppermute | solution.py:14
  127.3 0.9 collective-permute-done.2
  128.2 3.3 %collective-permute-done.3 = f32[32,2,512]{2,1,0:T(2,128)S(1)} collective-permute-done((f32[32,2,512]{2,1,0:T(2,128)S(1)}, f32[32,2,512]{2,1,0:T(2,128)S(1)}, u32[]{:S(2)}, u32[]{:S(2)}) %collective-permute-start.3) | collective-permute-done | bytes 131104 | tf_op jit(solution)/shard_map/ppermute | solution.py:14
  131.5 1.7 %fusion.25 = f32[32,4,512]{2,1,0:T(4,128)} fusion(f32[32,4,512]{2,1,0:T(4,128)S(1)} %copy.97, f32[32,2,512]{2,1,0:T(2,128)S(1)} %collective-permute-done.2, f32[32,2,512]{2,1,0:T(2,128)S(1)} %collective-permute-done.3, f32[32,4,2]{2,1,0:T(4,128)S(1)} %get-tuple-element.34, f32[32,4,510]{2,1,0:T(4,128)S(1)} %get-tuple-element.36, ...), kind=kLoop, calls=%fused_computation.51 | loop fusion | flops 2097152 | bytes 1859584 | tf_op jit(solution)/shard_map/add | solution.py:37
  (63 shorter events, 6.2 us)
Async XLA Ops:
  1.1 15.4 %collective-permute-start = (f32[35,4,512]{2,1,0:T(4,128)S(1)}, f32[35,4,512]{2,1,0:T(4,128)S(1)}, u32[]{:S(2)}, u32[]{:S(2)}) collective-permute-start(f32[35,4,512]{2,1,0:T(4,128)S(1)} %pad_maximum_fusion.11), channel_id=1, source_target_pairs={{0,4},{4,8},{8,12},{12,16},{16,20},{20,24},{24,28},{1,5},{5,9},{9,... | collective-permute-start | bytes 860168 | tf_op jit(solution)/shard_map/ppermute | solution.py:14
  4.5 14.1 %collective-permute-start.1 = (f32[35,4,512]{2,1,0:T(4,128)S(1)}, f32[35,4,512]{2,1,0:T(4,128)S(1)}, u32[]{:S(2)}, u32[]{:S(2)}) collective-permute-start(f32[35,4,512]{2,1,0:T(4,128)S(1)} %pad_maximum_fusion.11), channel_id=1, source_target_pairs={{4,0},{8,4},{12,8},{16,12},{20,16},{24,20},{28,24},{5,1},{9,5},{13... | collective-permute-start | bytes 860168 | tf_op jit(solution)/shard_map/ppermute | solution.py:17
  20.1 1.0 copy-start
  20.1 0.9 copy-start.1
  20.1 0.9 copy-start.2
  20.1 0.9 copy-start.3
  30.6 9.4 %all-to-all-start = ((f32[32,4,512]{2,0,1:T(8,128)}), f32[32,4,512]{2,0,1:T(8,128)S(1)}, u32[]{:S(2)}, u32[]{:S(2)}) async-start(f32[32,4,512]{2,0,1:T(8,128)} %copy.82), calls=%async_computation | async-start | bytes 524288 | tf_op jit(solution)/shard_map/all_to_all | solution.py:84
  49.6 6.8 %copy-start.4 = (s32[2,512]{1,0:T(2,128)S(1)}, s32[2,512]{1,0:T(2,128)}, u32[]{:S(2)}) copy-start(s32[2,512]{1,0:T(2,128)} %param.15) | copy-start | bytes 12292
  49.6 6.8 %copy-start.5 = (f32[2,512]{1,0:T(2,128)S(1)}, f32[2,512]{1,0:T(2,128)}, u32[]{:S(2)}) copy-start(f32[2,512]{1,0:T(2,128)} %param.16) | copy-start | bytes 12292
  49.6 6.9 %copy-start.6 = (f32[2,512]{1,0:T(2,128)S(1)}, f32[2,512]{1,0:T(2,128)}, u32[]{:S(2)}) copy-start(f32[2,512]{1,0:T(2,128)} %param.17) | copy-start | bytes 12292
  104.9 9.4 %all-to-all-start.1 = ((f32[128,1,512]{2,1,0:T(1,128)}), f32[128,1,512]{2,1,0:T(1,128)S(1)}, u32[]{:S(2)}, u32[]{:S(2)}) async-start(f32[128,1,512]{2,1,0:T(1,128)} %copy.91), calls=%async_computation.1 | async-start | bytes 524288 | tf_op jit(solution)/shard_map/all_to_all | solution.py:90
  121.4 6.9 %collective-permute-start.2 = (f32[32,2,512]{2,1,0:T(2,128)S(1)}, f32[32,2,512]{2,1,0:T(2,128)S(1)}, u32[]{:S(2)}, u32[]{:S(2)}) collective-permute-start(f32[32,2,512]{2,1,0:T(2,128)S(1)} %get-tuple-element.38), channel_id=1, source_target_pairs={{4,0},{8,4},{12,8},{16,12},{20,16},{24,20},{28,24},{5,1},{9,5},{13... | collective-permute-start | bytes 393224 | tf_op jit(solution)/shard_map/ppermute | solution.py:17
  123.8 7.8 %collective-permute-start.3 = (f32[32,2,512]{2,1,0:T(2,128)S(1)}, f32[32,2,512]{2,1,0:T(2,128)S(1)}, u32[]{:S(2)}, u32[]{:S(2)}) collective-permute-start(f32[32,2,512]{2,1,0:T(2,128)S(1)} %get-tuple-element.37), channel_id=1, source_target_pairs={{0,4},{4,8},{8,12},{12,16},{16,20},{20,24},{24,28},{1,5},{5,9},{9,... | collective-permute-start | bytes 393224 | tf_op jit(solution)/shard_map/ppermute | solution.py:14
where the time goes:
time: 134 us; the launch traced here: 133 us
  other arithmetic  58.6 us (44%)
  local copies, waits for them, and re-layouts  32.9 us (25%)
  starting transfers between devices  19.6 us (15%)
  waiting for transfers between devices  18 us (13%)
  matrix products  3.7 us (3%)
    another operation x3, other arithmetic, analyze(): factor = jnp.linalg.cholesky(system)  23.6 us
    another operation x3, other arithmetic, analyze(): solved = jax.scipy.linalg.cho_solve((factor, True), right_side)  19.8 us
    gather x2, local copies, waits for them, and re-layouts, analyze(): innovation = observed - jnp.take(center, cells)  9.12 us
    ppermute x2, starting transfers between devices, extended(): lax.ppermute(lax.slice_in_dim(block, block.shape[dim] - width, None, axis...  6.86 us
    gather x1, local copies, waits for them, and re-layouts, analyze(): obs_spread = jnp.take(spread, cells, axis=1)  6.79 us
    all_to_all x1, waiting for transfers between devices, on_device(): lax.all_to_all(outgoing, 'mem', split_axis=0, concat_axis=1, tiled=True)  5.96 us
    all_to_all x1, waiting for transfers between devices, on_device(): lax.all_to_all(blocks, 'mem', split_axis=1, concat_axis=0, tiled=True)  5.78 us
    sort x1, other arithmetic, on_device(): positions = jnp.argsort(order)  5.74 us
  transfers between devices with their start and end apart: 6, of which 5 were waited for; matrix products, arithmetic and copies ran while one was open for 7% of the time, Pallas kernels for 0%

commit v1 on v0

--- a/solution.py
+++ b/solution.py
@@ -1,9 +1,26 @@
+import functools
 import jax
 import jax.numpy as jnp
 from jax import lax
 from jax.sharding import PartitionSpec as P
 
 PATCH = 256
+
+
+def show_hubs(xin, at_axis, dim_i):
+    latest = jnp.concatenate(
+        lax.all_to_all(
+            jnp.stack(jnp.split(xin, lax.axis_size("mem"), axis=at_axis), axis=0),
+            axis_name="mem",
+            concat_axis=0,
+            split_axis=0,
+        ),
+        axis=dim_i,
+    )
+    return latest
+
+
+lay_the_vector = functools.partial(show_hubs, at_axis=1, dim_i=0)
 
 
 def extended(block, sides, width):
@@ -81,7 +98,7 @@
     order = assign[0]
     permuted = jnp.take(ensemble.reshape(local_members, columns), order, axis=1)
     blocks = permuted.reshape(local_members, groups, group_columns)
-    gathered = lax.all_to_all(blocks, "mem", split_axis=1, concat_axis=0, tiled=True)
+    gathered = lay_the_vector(blocks)
     gathered = gathered.reshape(local_members * groups, patches_here, PATCH)
     updated = jax.vmap(analyze, in_axes=(1, 0, 0, 0), out_axes=1)(
         gathered, obs_cell, obs_value, obs_var

time: 134 us -> 134 us (level)
  no operation moved by 1% of the time
where the time goes in v1:
time: 134 us; the launch traced here: 133 us
  other arithmetic  59.4 us (44%)
  local copies, waits for them, and re-layouts  32.4 us (24%)
  starting transfers between devices  19.6 us (15%)
  waiting for transfers between devices  18 us (13%)
  matrix products  3.69 us (3%)
    another operation x3, other arithmetic, analyze(): factor = jnp.linalg.cholesky(system)  23.6 us
    another operation x3, other arithmetic, analyze(): solved = jax.scipy.linalg.cho_solve((factor, True), right_side)  19.8 us
    gather x2, local copies, waits for them, and re-layouts, analyze(): innovation = observed - jnp.take(center, cells)  9.12 us
    ppermute x2, starting transfers between devices, extended(): lax.ppermute(lax.slice_in_dim(block, block.shape[dim] - width, None, axis...  6.85 us
    gather x1, local copies, waits for them, and re-layouts, analyze(): obs_spread = jnp.take(spread, cells, axis=1)  6.79 us
    all_to_all x1, waiting for transfers between devices, on_device(): lax.all_to_all(outgoing, 'mem', split_axis=0, concat_axis=1, tiled=True)  5.96 us
    all_to_all x1, waiting for transfers between devices, show_hubs(): lax.all_to_all(jnp.stack(jnp.split(xin, lax.axis_size('mem'), axis=at_axi...  5.78 us
    sort x1, other arithmetic, on_device(): positions = jnp.argsort(order)  5.74 us
  transfers between devices with their start and end apart: 6, of which 5 were waited for; matrix products, arithmetic and copies ran while one was open for 7% of the time, Pallas kernels for 0%

profile of v1, /device:TPU:24, one launch (start us, length us, event | category | flops | bytes accessed | tf_op | source)
XLA Modules:
  0.0 133.5 jit_solution(9395561147611919042)
XLA Ops:
  0.0 1.1 pad_maximum_fusion.11
  1.1 3.4 %collective-permute-start = (f32[35,4,512]{2,1,0:T(4,128)S(1)}, f32[35,4,512]{2,1,0:T(4,128)S(1)}, u32[]{:S(2)}, u32[]{:S(2)}) collective-permute-start(f32[35,4,512]{2,1,0:T(4,128)S(1)} %pad_maximum_fusion.11), channel_id=1, source_target_pairs={{0,4},{4,8},{8,12},{12,16},{16,20},{20,24},{24,28},{1,5},{5,9},{9,... | collective-permute-start | bytes 860168 | tf_op jit(solution)/shard_map/ppermute | solution.py:31
  4.5 3.3 %collective-permute-start.1 = (f32[35,4,512]{2,1,0:T(4,128)S(1)}, f32[35,4,512]{2,1,0:T(4,128)S(1)}, u32[]{:S(2)}, u32[]{:S(2)}) collective-permute-start(f32[35,4,512]{2,1,0:T(4,128)S(1)} %pad_maximum_fusion.11), channel_id=1, source_target_pairs={{4,0},{8,4},{12,8},{16,12},{20,16},{24,20},{28,24},{5,1},{9,5},{13... | collective-permute-start | bytes 860168 | tf_op jit(solution)/shard_map/ppermute | solution.py:34
  7.8 0.7 fusion.66
  8.5 0.7 compare_and_fusion.1
  9.3 0.7 fusion.68
  10.0 5.7 %sort.17 = (s32[2048]{0:T(1024)}, s32[2048]{0:T(1024)S(1)}) sort(s32[2048]{0:T(1024)} %bitcast.93, s32[2048]{0:T(1024)S(1)} %iota.82), dimensions={0}, to_apply=%region_3.5 | sort | flops 22528 | bytes 32768 | tf_op jit(solution)/shard_map/jit(argsort)/sort | solution.py:109
  15.8 0.7 broadcast_multiply_fusion
  16.5 2.1 %collective-permute-done.1 = f32[35,4,512]{2,1,0:T(4,128)S(1)} collective-permute-done((f32[35,4,512]{2,1,0:T(4,128)S(1)}, f32[35,4,512]{2,1,0:T(4,128)S(1)}, u32[]{:S(2)}, u32[]{:S(2)}) %collective-permute-start.1) | collective-permute-done | bytes 286752 | tf_op jit(solution)/shard_map/ppermute | solution.py:34
  18.6 1.2 pad_maximum_fusion
  21.1 0.9 fusion.6
  22.6 0.8 fusion.29
  23.7 5.5 %gather_fusion.2 = f32[2048,32]{1,0:T(8,128)S(1)} fusion(f32[32,2048]{0,1:T(8,128)S(1)} %bitcast.67, s32[2048]{0:T(1024)S(1)} %fusion.66), kind=kCustom, calls=%fused_computation.clone | custom fusion | bytes 532480 | tf_op jit(solution)/shard_map/jit(_take)/gather | solution.py:99
  30.1 0.7 pad_maximum_fusion.16
  30.8 3.6 %all-to-all-start = ((f32[4,32,1,512]{3,1,2,0:T(8,128)}), f32[4,32,1,512]{3,1,2,0:T(8,128)S(1)}, u32[]{:S(2)}, u32[]{:S(2)}) async-start(f32[4,32,1,512]{3,1,2,0:T(8,128)} %pad_maximum_fusion.16), calls=%async_computation | async-start | bytes 524288 | tf_op jit(solution)/shard_map/all_to_all | solution.py:12
  34.4 5.8 %all-to-all-done = f32[4,32,1,512]{3,1,2,0:T(8,128)S(1)} async-done(((f32[4,32,1,512]{3,1,2,0:T(8,128)}), f32[4,32,1,512]{3,1,2,0:T(8,128)S(1)}, u32[]{:S(2)}, u32[]{:S(2)}) %all-to-all-start) | async-done | bytes 262176 | tf_op jit(solution)/shard_map/all_to_all | solution.py:12
  40.7 9.1 %gather_fusion.1 = f32[1024]{0:T(1024)S(1)} fusion(f32[2,256]{1,0:T(2,128)S(1)} %div.32, s32[1024]{0:T(1024)S(1)} %bitcast.65), kind=kCustom, calls=%fused_computation.3 | custom fusion | bytes 16384 | tf_op jit(solution)/shard_map/vmap(jit(_take))/gather | solution.py:63
  49.9 6.8 %gather_fusion = f32[1024,128]{1,0:T(8,128)S(1)} fusion(f32[2,128,256]{1,2,0:T(8,128)S(1)} %subtract_bitcast_fusion, s32[1024]{0:T(1024)S(1)} %bitcast.66), kind=kCustom, calls=%fused_computation.2 | custom fusion | bytes 1056768 | tf_op jit(solution)/shard_map/vmap(jit(_take))/gather | solution.py:62
  56.7 1.8 %fusion.14 = f32[2,128,128]{1,2,0:T(8,128)S(1)} fusion(f32[2,512,128]{2,1,0:T(8,128)S(1)} %bitcast.73, f32[2,512]{1,0:T(2,128)S(1)} %copy-done.6, pred[2,512]{1,0:T(4,128)(4,1)S(1)} %get-tuple-element.9), kind=kOutput, calls=%fused_computation.38 | convolution fusion | flops 201719808 | bytes 660480 | tf_op jit(solution)/shard_map/vmap()/dot_general | solution.py:65
  58.7 23.5 %custom-call.11 = f32[2,128,128]{2,1,0:T(8,128)S(1)} custom-call(f32[2,128,128]{2,1,0:T(8,128)S(1)} %fusion.54), custom_call_target="Cholesky" | custom-call | tf_op jit(solution)/shard_map/vmap(jit(cholesky))/cholesky | solution.py:67
  82.4 19.7 %custom-call.12 = f32[2,1,128,128]{2,3,1,0:T(8,128)S(1)} custom-call(f32[2,1,128,128]{3,2,1,0:T(8,128)S(1)} %select_bitcast_fusion), custom_call_target="InvertDiagBlocksLowerTriangular" | custom-call | tf_op jit(solution)/shard_map/vmap(jit(_cho_solve))/triangular_solve | solution.py:70
  102.1 0.6 convolution_bitcast_fusion
  103.6 0.5 fusion
  104.2 0.8 copy.100
  105.1 3.4 %all-to-all-start.1 = ((f32[128,1,512]{2,1,0:T(1,128)}), f32[128,1,512]{2,1,0:T(1,128)S(1)}, u32[]{:S(2)}, u32[]{:S(2)}) async-start(f32[128,1,512]{2,1,0:T(1,128)} %copy.100), calls=%async_computation.1 | async-start | bytes 524288 | tf_op jit(solution)/shard_map/all_to_all | solution.py:107
  108.5 6.0 %all-to-all-done.1 = f32[128,1,512]{2,1,0:T(1,128)S(1)} async-done(((f32[128,1,512]{2,1,0:T(1,128)}), f32[128,1,512]{2,1,0:T(1,128)S(1)}, u32[]{:S(2)}, u32[]{:S(2)}) %all-to-all-start.1) | async-done | bytes 262176 | tf_op jit(solution)/shard_map/all_to_all | solution.py:107
  114.8 5.5 %gather_fusion.3 = f32[2048,32]{1,0:T(8,128)S(1)} fusion(f32[32,2048]{0,1:T(8,128)S(1)} %bitcast.68, s32[2048]{0:T(1024)S(1)} %fusion.67), kind=kCustom, calls=%fused_computation.1.clone | custom fusion | bytes 532480 | tf_op jit(solution)/shard_map/jit(_take)/gather | solution.py:110
  121.6 2.4 %collective-permute-start.2 = (f32[32,2,512]{2,1,0:T(2,128)S(1)}, f32[32,2,512]{2,1,0:T(2,128)S(1)}, u32[]{:S(2)}, u32[]{:S(2)}) collective-permute-start(f32[32,2,512]{2,1,0:T(2,128)S(1)} %get-tuple-element.42), channel_id=1, source_target_pairs={{4,0},{8,4},{12,8},{16,12},{20,16},{24,20},{28,24},{5,1},{9,5},{13... | collective-permute-start | bytes 393224 | tf_op jit(solution)/shard_map/ppermute | solution.py:34
  124.0 3.5 %collective-permute-start.3 = (f32[32,2,512]{2,1,0:T(2,128)S(1)}, f32[32,2,512]{2,1,0:T(2,128)S(1)}, u32[]{:S(2)}, u32[]{:S(2)}) collective-permute-start(f32[32,2,512]{2,1,0:T(2,128)S(1)} %get-tuple-element.41), channel_id=1, source_target_pairs={{0,4},{4,8},{8,12},{12,16},{16,20},{20,24},{24,28},{1,5},{5,9},{9,... | collective-permute-start | bytes 393224 | tf_op jit(solution)/shard_map/ppermute | solution.py:31
  127.6 0.9 collective-permute-done.2
  128.5 3.3 %collective-permute-done.3 = f32[32,2,512]{2,1,0:T(2,128)S(1)} collective-permute-done((f32[32,2,512]{2,1,0:T(2,128)S(1)}, f32[32,2,512]{2,1,0:T(2,128)S(1)}, u32[]{:S(2)}, u32[]{:S(2)}) %collective-permute-start.3) | collective-permute-done | bytes 131104 | tf_op jit(solution)/shard_map/ppermute | solution.py:31
  131.8 1.7 %fusion.25 = f32[32,4,512]{2,1,0:T(4,128)} fusion(f32[32,4,512]{2,1,0:T(4,128)S(1)} %copy.106, f32[32,2,512]{2,1,0:T(2,128)S(1)} %collective-permute-done.2, f32[32,2,512]{2,1,0:T(2,128)S(1)} %collective-permute-done.3, f32[32,4,2]{2,1,0:T(4,128)S(1)} %get-tuple-element.38, f32[32,4,510]{2,1,0:T(4,128)S(1)} %get-tuple-element.40, ...), kind=kLoop, calls=%fused_computation.51 | loop fusion | flops 2097152 | bytes 1859584 | tf_op jit(solution)/shard_map/add | solution.py:54
  (68 shorter events, 6.7 us)
Async XLA Ops:
  1.1 15.4 %collective-permute-start = (f32[35,4,512]{2,1,0:T(4,128)S(1)}, f32[35,4,512]{2,1,0:T(4,128)S(1)}, u32[]{:S(2)}, u32[]{:S(2)}) collective-permute-start(f32[35,4,512]{2,1,0:T(4,128)S(1)} %pad_maximum_fusion.11), channel_id=1, source_target_pairs={{0,4},{4,8},{8,12},{12,16},{16,20},{20,24},{24,28},{1,5},{5,9},{9,... | collective-permute-start | bytes 860168 | tf_op jit(solution)/shard_map/ppermute | solution.py:31
  4.5 14.1 %collective-permute-start.1 = (f32[35,4,512]{2,1,0:T(4,128)S(1)}, f32[35,4,512]{2,1,0:T(4,128)S(1)}, u32[]{:S(2)}, u32[]{:S(2)}) collective-permute-start(f32[35,4,512]{2,1,0:T(4,128)S(1)} %pad_maximum_fusion.11), channel_id=1, source_target_pairs={{4,0},{8,4},{12,8},{16,12},{20,16},{24,20},{28,24},{5,1},{9,5},{13... | collective-permute-start | bytes 860168 | tf_op jit(solution)/shard_map/ppermute | solution.py:34
  20.1 1.0 copy-start
  20.1 0.9 copy-start.1
  20.1 0.9 copy-start.2
  20.1 0.9 copy-start.3
  30.8 9.4 %all-to-all-start = ((f32[4,32,1,512]{3,1,2,0:T(8,128)}), f32[4,32,1,512]{3,1,2,0:T(8,128)S(1)}, u32[]{:S(2)}, u32[]{:S(2)}) async-start(f32[4,32,1,512]{3,1,2,0:T(8,128)} %pad_maximum_fusion.16), calls=%async_computation | async-start | bytes 524288 | tf_op jit(solution)/shard_map/all_to_all | solution.py:12
  49.8 6.8 %copy-start.4 = (s32[2,512]{1,0:T(2,128)S(1)}, s32[2,512]{1,0:T(2,128)}, u32[]{:S(2)}) copy-start(s32[2,512]{1,0:T(2,128)} %param.15) | copy-start | bytes 12292
  49.8 6.8 %copy-start.5 = (f32[2,512]{1,0:T(2,128)S(1)}, f32[2,512]{1,0:T(2,128)}, u32[]{:S(2)}) copy-start(f32[2,512]{1,0:T(2,128)} %param.16) | copy-start | bytes 12292
  49.9 6.9 %copy-start.6 = (f32[2,512]{1,0:T(2,128)S(1)}, f32[2,512]{1,0:T(2,128)}, u32[]{:S(2)}) copy-start(f32[2,512]{1,0:T(2,128)} %param.17) | copy-start | bytes 12292
  105.1 9.4 %all-to-all-start.1 = ((f32[128,1,512]{2,1,0:T(1,128)}), f32[128,1,512]{2,1,0:T(1,128)S(1)}, u32[]{:S(2)}, u32[]{:S(2)}) async-start(f32[128,1,512]{2,1,0:T(1,128)} %copy.100), calls=%async_computation.1 | async-start | bytes 524288 | tf_op jit(solution)/shard_map/all_to_all | solution.py:107
  121.6 6.9 %collective-permute-start.2 = (f32[32,2,512]{2,1,0:T(2,128)S(1)}, f32[32,2,512]{2,1,0:T(2,128)S(1)}, u32[]{:S(2)}, u32[]{:S(2)}) collective-permute-start(f32[32,2,512]{2,1,0:T(2,128)S(1)} %get-tuple-element.42), channel_id=1, source_target_pairs={{4,0},{8,4},{12,8},{16,12},{20,16},{24,20},{28,24},{5,1},{9,5},{13... | collective-permute-start | bytes 393224 | tf_op jit(solution)/shard_map/ppermute | solution.py:34
  124.0 7.8 %collective-permute-start.3 = (f32[32,2,512]{2,1,0:T(2,128)S(1)}, f32[32,2,512]{2,1,0:T(2,128)S(1)}, u32[]{:S(2)}, u32[]{:S(2)}) collective-permute-start(f32[32,2,512]{2,1,0:T(2,128)S(1)} %get-tuple-element.41), channel_id=1, source_target_pairs={{0,4},{4,8},{8,12},{12,16},{16,20},{20,24},{24,28},{1,5},{5,9},{9,... | collective-permute-start | bytes 393224 | tf_op jit(solution)/shard_map/ppermute | solution.py:31
